TPU v7x, 512 devices: a whole 4x4x16 slice. The times are simulated.
512 devices in a mesh: rep: 16 (over x, z_lo), mp: 32 (over z_hi, y, core).
Axes of the slice: x: 4, y: 4, z: 16 (z_hi: 4, z_lo: 4; z = z_hi * 4 + z_lo), core: 2. Of those that a mesh axis runs over, the one named last changes fastest.
Arguments:
- dense_feats: bfloat16 [65536, 13], P(('rep', 'mp')), may hold values from -6 to 6
- bag_counts: int32 [65536, 32, 64], P('rep', 'mp'), may hold values from 0 to 2
- emb_rows: bfloat16 [32, 64, 256], P('mp'), may hold values from -0.625 to 0.625
- v_emb: bfloat16 [8192, 256], P('mp'), may hold values from -0.0625 to 0.0625
- u_emb: bfloat16 [256, 8192], P(None, 'mp'), may hold values from -0.375 to 0.375
- b_emb: bfloat16 [8192], P('mp'), may hold values from -3 to 3
- v_bot: bfloat16 [256, 256], replicated, may hold values from -0.375 to 0.375
- u_bot: bfloat16 [256, 256], replicated, may hold values from -0.375 to 0.375
- b_bot: bfloat16 [256], replicated, may hold values from -3 to 3
- w_first: bfloat16 [13, 1024], replicated, may hold values from -1.75 to 1.75
- b_first: bfloat16 [1024], replicated, may hold values from -3 to 3
- w_second: bfloat16 [1024, 256], replicated, may hold values from -0.1875 to 0.1875
- b_second: bfloat16 [256], replicated, may hold values from -3 to 3
- cot_cross: bfloat16 [65536, 8192], P(('rep', 'mp')), may hold values from -24 to 24
- cot_bottom: bfloat16 [65536, 256], P(('rep', 'mp')), may hold values from -6 to 6
Outputs:
- cross_emb: bfloat16 [65536, 8192], P(('rep', 'mp'))
- cross_bot: bfloat16 [65536, 256], P(('rep', 'mp'))
- grad_table: bfloat16 [32, 64, 256], P('mp')
- grad_v_emb: bfloat16 [8192, 256], P('mp')
- grad_u_emb: bfloat16 [256, 8192], P(None, 'mp')
- grad_b_emb: bfloat16 [8192], P('mp')
- grad_v_bot: bfloat16 [256, 256], replicated
- grad_u_bot: bfloat16 [256, 256], replicated
- grad_b_bot: bfloat16 [256], replicated
- grad_w_first: bfloat16 [13, 1024], replicated
- grad_b_first: bfloat16 [1024], replicated
- grad_w_second: bfloat16 [1024, 256], replicated
- grad_b_second: bfloat16 [256], replicated
Inputs may be any that keep to these rules, and one draw needn't show every extreme that they name: bag_counts[s, t, j] is how often row j of table t occurs in the bag of sample s.
All inputs are finite; a program needn't handle non-finite values.
Results may differ from a plain program's by a relative error of at most 0.029.
Values may be sent and summed in bfloat16 or wider, within the bound.
A program may use at most 64 MiB of HBM per device.

v0:
```python
import math
import jax
import jax.numpy as jnp
from jax import lax
from jax.sharding import PartitionSpec as P


def silu_slope(inputs):
    gate_value = jax.nn.sigmoid(inputs)
    return gate_value * (1.0 + inputs * (1.0 - gate_value))


def contract_rows(left_side, right_side):
    return lax.dot_general(
        left_side, right_side, (((0,), (0,)), ((), ())), preferred_element_type=jnp.float32
    )


def contract_cols(left_side, right_side):
    return lax.dot_general(
        left_side, right_side, (((1,), (1,)), ((), ())), preferred_element_type=jnp.float32
    )


def local(
    dense_feats,
    bag_counts,
    emb_rows,
    v_emb,
    u_emb,
    b_emb,
    v_bot,
    u_bot,
    b_bot,
    w_first,
    b_first,
    w_second,
    b_second,
    cot_cross,
    cot_bottom,
):
    group_size = lax.axis_size("mp")
    own_rows = dense_feats.shape[0]
    first_row = lax.axis_index("mp") * own_rows
    grad_scale = 1.0 / math.sqrt(own_rows * group_size * lax.axis_size("rep"))
    counts = bag_counts[:, 0, :].astype(jnp.bfloat16)
    pooled = jnp.dot(counts, emb_rows[0], preferred_element_type=jnp.float32).astype(jnp.bfloat16)
    partial_value = jnp.dot(pooled, v_emb, preferred_element_type=jnp.float32)
    first_pre = jnp.dot(dense_feats, w_first, preferred_element_type=jnp.float32) + b_first.astype(
        jnp.float32
    )
    first_act = jax.nn.silu(first_pre).astype(jnp.bfloat16)
    second_pre = jnp.dot(first_act, w_second, preferred_element_type=jnp.float32) + b_second.astype(
        jnp.float32
    )
    bottom = jax.nn.silu(second_pre).astype(jnp.bfloat16)
    own_part = lax.dynamic_slice_in_dim(partial_value, first_row, own_rows, 0) + jnp.dot(
        bottom, v_bot, preferred_element_type=jnp.float32
    )
    partial_value = lax.dynamic_update_slice_in_dim(partial_value, own_part, first_row, 0)
    low_rank = lax.psum(partial_value.astype(jnp.bfloat16), "mp")
    lift_emb = jnp.dot(low_rank, u_emb, preferred_element_type=jnp.float32) + b_emb.astype(
        jnp.float32
    )
    pooled_full = pooled.astype(jnp.float32)
    cross_local = (pooled_full * (lift_emb + 1.0)).astype(jnp.bfloat16)
    cross_emb = lax.all_to_all(cross_local, "mp", split_axis=0, concat_axis=1, tiled=True)
    own_low = lax.dynamic_slice_in_dim(low_rank, first_row, own_rows, 0)
    lift_bottom = jnp.dot(own_low, u_bot, preferred_element_type=jnp.float32) + b_bot.astype(
        jnp.float32
    )
    bottom_full = bottom.astype(jnp.float32)
    cross_bot = (bottom_full * (lift_bottom + 1.0)).astype(jnp.bfloat16)
    cot_rows = lax.all_to_all(cot_cross, "mp", split_axis=1, concat_axis=0, tiled=True).astype(
        jnp.float32
    )
    d_lift = cot_rows * pooled_full
    d_lift_round = d_lift.astype(jnp.bfloat16)
    own_back = lax.psum_scatter(
        contract_cols(d_lift_round, u_emb).astype(jnp.bfloat16),
        "mp",
        scatter_dimension=0,
        tiled=True,
    ).astype(jnp.float32)
    cot_low = cot_bottom.astype(jnp.float32)
    d_bottom_lift = cot_low * bottom_full
    d_bottom_round = d_bottom_lift.astype(jnp.bfloat16)
    own_d_low = (own_back + contract_cols(d_bottom_round, u_bot)).astype(jnp.bfloat16)
    d_low = lax.all_gather(own_d_low, "mp", axis=0, tiled=True)
    d_pooled = (cot_rows * (lift_emb + 1.0) + contract_cols(d_low, v_emb)).astype(jnp.bfloat16)
    grad_table = grad_scale * contract_rows(counts, d_pooled)
    grad_v = grad_scale * contract_rows(pooled, d_low)
    grad_u = grad_scale * contract_rows(low_rank, d_lift_round)
    grad_b = grad_scale * jnp.sum(d_lift, axis=0)
    d_bottom = cot_low * (lift_bottom + 1.0) + contract_cols(own_d_low, v_bot)
    grad_vb = grad_scale * contract_rows(bottom, own_d_low)
    grad_ub = grad_scale * contract_rows(own_low, d_bottom_round)
    grad_bb = grad_scale * jnp.sum(d_bottom_lift, axis=0)
    d_second = d_bottom * silu_slope(second_pre)
    d_second_round = d_second.astype(jnp.bfloat16)
    grad_ws = grad_scale * contract_rows(first_act, d_second_round)
    grad_bs = grad_scale * jnp.sum(d_second, axis=0)
    d_first = contract_cols(d_second_round, w_second) * silu_slope(first_pre)
    d_first_round = d_first.astype(jnp.bfloat16)
    grad_wf = grad_scale * contract_rows(dense_feats, d_first_round)
    grad_bf = grad_scale * jnp.sum(d_first, axis=0)
    dense_sums = lax.psum(
        (grad_wf, grad_bf, grad_ws, grad_bs, grad_vb, grad_ub, grad_bb), ("rep", "mp")
    )
    table_sums = (
        lax.psum(grad_table.astype(jnp.bfloat16), "rep").astype(jnp.float32),
        lax.psum(grad_v.astype(jnp.bfloat16), "rep").astype(jnp.float32),
        lax.psum(grad_u.astype(jnp.bfloat16), "rep").astype(jnp.float32),
        lax.psum(grad_b.astype(jnp.bfloat16), "rep").astype(jnp.float32),
    )
    return (
        cross_emb,
        cross_bot,
        table_sums[0][None].astype(jnp.bfloat16),
        table_sums[1].astype(jnp.bfloat16),
        table_sums[2].astype(jnp.bfloat16),
        table_sums[3].astype(jnp.bfloat16),
        dense_sums[4].astype(jnp.bfloat16),
        dense_sums[5].astype(jnp.bfloat16),
        dense_sums[6].astype(jnp.bfloat16),
        dense_sums[0].astype(jnp.bfloat16),
        dense_sums[1].astype(jnp.bfloat16),
        dense_sums[2].astype(jnp.bfloat16),
        dense_sums[3].astype(jnp.bfloat16),
    )


def solution(mesh):
    return jax.shard_map(
        local,
        mesh=mesh,
        in_specs=(
            P(("rep", "mp"), None),
            P("rep", "mp", None),
            P("mp", None, None),
            P("mp", None),
            P(None, "mp"),
            P("mp"),
            P(),
            P(),
            P(),
            P(),
            P(),
            P(),
            P(),
            P(("rep", "mp"), None),
            P(("rep", "mp"), None),
        ),
        out_specs=(
            P(("rep", "mp"), None),
            P(("rep", "mp"), None),
            P("mp", None, None),
            P("mp", None),
            P(None, "mp"),
            P("mp"),
            P(),
            P(),
            P(),
            P(),
            P(),
            P(),
            P(),
        ),
        check_vma=False,
    )
```

profile of v0, /device:TPU:8, one launch (start us, length us, event | category | flops | bytes accessed | tf_op | source)
XLA Modules:
  0.0 923.8 jit_solution(9754976400988497330)
XLA Ops:
  7.2 0.0 copy-start
  7.2 3.2 copy.33
  10.4 0.0 copy-start.8
  10.4 18.5 %all-to-all-start.1 = ((bf16[128,32,256]{2,0,1:T(8,128)(2,1)}), bf16[128,32,256]{2,0,1:T(8,128)(2,1)}, u32[]{:S(2)}, u32[]{:S(2)}) async-start(bf16[128,32,256]{2,0,1:T(8,128)(2,1)} %bitcast.58), calls=%async_computation.1 | async-start | bytes 4194304 | tf_op jit(solution)/shard_map/all_to_all | solution.py:74
  29.0 0.0 copy-start.11
  29.0 0.0 all-reduce.7.cloned.1.call-start
  29.0 0.0 copy-done.15
  29.1 0.0 copy-done.14
  29.1 0.0 copy-done.12
  29.1 0.0 copy-done.13
  29.1 0.3 convolution_add_fusion.2
  29.4 0.0 copy-start.5
  29.4 0.8 copy-done.5
  30.2 0.0 copy-done
  30.2 0.0 copy-done.8
  30.2 1.0 fusion.22
  31.1 0.0 copy-done.11
  31.1 2.0 convolution_convert_fusion.1
  33.1 0.0 copy-start.9
  33.1 0.7 fusion.35
  33.9 0.2 copy-done.9
  34.0 0.2 fusion.8
  34.2 1.5 convert_element_type.134
  35.8 0.0 all-reduce.7.cloned.1.call-update
  35.8 0.0 reduce-scatter.2.cloned.1.call-start
  35.8 0.6 copy-done.16
  36.4 399.7 %all-reduce.7.cloned.1.call-done = bf16[4096,256]{1,0:T(8,128)(2,1)} async-done(((bf16[4096,256]{1,0:T(8,128)(2,1)}), bf16[4096,256]{1,0:T(8,128)(2,1)}) %all-reduce.7.cloned.1.call-update) | async-done | bytes 2097168 | tf_op jit(solution)/shard_map/psum | solution.py:61
  436.1 0.0 all-to-all-done.1
  436.1 6.4 bitcast_multiply_fusion
  442.6 1.3 copy-done.1
  443.9 2.1 convolution_convert_fusion
  446.0 0.0 reduce-scatter.2.cloned.1.call-update
  446.0 0.0 copy-start.7
  446.1 0.0 copy-start.17
  446.1 21.6 %all-to-all-start = ((bf16[32,128,256]{2,1,0:T(8,128)(2,1)}), bf16[32,128,256]{2,1,0:T(8,128)(2,1)}, u32[]{:S(2)}, u32[]{:S(2)}) async-start(bf16[32,128,256]{2,1,0:T(8,128)(2,1)} %bitcast.59), calls=%async_computation | async-start | bytes 4194304 | tf_op jit(solution)/shard_map/all_to_all | solution.py:67
  467.7 0.0 all-gather.2.cloned.1.call-start
  467.7 151.9 %reduce-scatter.2.cloned.1.call-done = bf16[128,256]{1,0:T(8,128)(2,1)} async-done(((bf16[4096,256]{1,0:T(8,128)(2,1)}), bf16[128,256]{1,0:T(8,128)(2,1)}) %reduce-scatter.2.cloned.1.call-update) | async-done | bytes 65552 | tf_op jit(solution)/shard_map/reduce_scatter | solution.py:79
  619.7 0.0 copy-done.7
  619.7 1.7 fusion.11
  621.3 0.0 all-gather.2.cloned.1.call-update
  621.4 0.0 all-reduce.9.cloned.1.call-start
  621.4 0.0 copy-done.17
  621.4 1.1 convolution_multiply_fusion.2
  622.5 1.6 fusion.21
  624.2 0.0 copy-start.18
  624.2 0.0 copy-start.6
  624.2 3.7 fusion.7
  627.9 0.2 convolution_multiply_fusion.3
  628.1 0.0 copy-done.10
  628.1 0.0 copy-done.18
  628.1 0.2 fusion.34
  628.4 0.4 fusion.33
  628.7 0.2 fusion.13
  628.9 1.4 convolution_multiply_fusion
  630.3 114.5 %all-reduce.10 = (bf16[256,256]{1,0:T(8,128)(2,1)}, bf16[256,256]{1,0:T(8,128)(2,1)}, bf16[256]{0:T(256)(128)(2,1)}, bf16[13,1024]{1,0:T(8,128)(2,1)}, bf16[1024...) all-reduce(f32[256,256]{1,0:T(8,128)S(1)} %convolution_multiply_fus, ...), channel_id=1, replica_groups=mesh['rep'=16,'mp'=32] {'rep','mp'}, use_global_device_ids=true, to_apply=%region_7.8 | all-reduce | flops 408064 | bytes 2448384 | tf_op jit(solution)/shard_map/psum | solution.py:107
  744.8 3.0 fusion.6
  747.8 0.0 all-reduce.9.cloned.1.call-update
  747.8 4.5 fusion.15
  752.3 78.6 %all-reduce.1 = (bf16[1,64,256]{2,1,0:T(8,128)(2,1)}, bf16[256]{0:T(256)(128)(2,1)}) all-reduce(bf16[1,64,256]{2,1,0:T(8,128)(2,1)S(1)} %fusion.15, bf16[256]{0:T(256)(128)(2,1)S(1)} %multiply_convert_fusion.2), channel_id=1, replica_groups=mesh['rep'=16,'mp'=32] {'rep'}, use_global_device_ids=true, to_apply=%region_2.3 | all-reduce | flops 16640 | bytes 66560 | tf_op jit(solution)/shard_map/psum | solution.py:111
  830.9 0.0 all-to-all-done
  830.9 3.1 copy.31
  834.0 80.1 %all-reduce.9.cloned.1.call-done = (bf16[256,256]{1,0:T(8,128)(2,1)}, bf16[256,256]{1,0:T(8,128)(2,1)}) async-done(((bf16[256,256]{1,0:T(8,128)(2,1)}, bf16[256,256]{1,0:T(8,128)(2,1)}), (bf16[256,256]{1,0:T(8,128)(2,1)}, bf16[256,256]{1,0:T(8,128)(2,1)})) %all-reduce.9.cloned.1.call-update) | async-done | bytes 262160 | tf_op jit(solution)/shard_map/psum | solution.py:112
  914.1 1.6 copy.52
  915.7 1.6 copy.53
  (23 shorter events, 0.1 us)
Async XLA Ops:
  7.2 23.0 %copy-start = (bf16[1024,256]{1,0:T(8,128)(2,1)S(1)}, bf16[1024,256]{1,0:T(8,128)(2,1)}, u32[]{:S(2)}) copy-start(bf16[1024,256]{1,0:T(8,128)(2,1)} %param.26) | copy-start | bytes 1572868
  10.4 18.6 %copy-start.15 = (bf16[256]{0:T(256)(128)(2,1)S(1)}, bf16[256]{0:T(256)(128)(2,1)}, u32[]{:S(2)}) copy-start(bf16[256]{0:T(256)(128)(2,1)} %param.27) | copy-start | bytes 1540
  10.4 18.6 %copy-start.14 = (bf16[1024]{0:T(1024)(128)(2,1)S(1)}, bf16[1024]{0:T(1024)(128)(2,1)}, u32[]{:S(2)}) copy-start(bf16[1024]{0:T(1024)(128)(2,1)} %param.25) | copy-start | bytes 6148
  10.4 18.7 %copy-start.12 = (bf16[13,1024]{1,0:T(8,128)(2,1)S(1)}, bf16[13,1024]{1,0:T(8,128)(2,1)}, u32[]{:S(2)}) copy-start(bf16[13,1024]{1,0:T(8,128)(2,1)} %param.24) | copy-start | bytes 79876
  10.4 18.7 %copy-start.13 = (bf16[128,13]{0,1:T(8,128)(2,1)S(1)}, bf16[128,13]{0,1:T(8,128)(2,1)}, u32[]{:S(2)}) copy-start(bf16[128,13]{0,1:T(8,128)(2,1)} %param.15) | copy-start | bytes 9988
  10.4 19.7 %copy-start.8 = (bf16[128,256]{1,0:T(8,128)(2,1)S(1)}, bf16[128,256]{1,0:T(8,128)(2,1)}, u32[]{:S(2)}) copy-start(bf16[128,256]{1,0:T(8,128)(2,1)} %param.29) | copy-start | bytes 196612
  10.4 425.7 %all-to-all-start.1 = ((bf16[128,32,256]{2,0,1:T(8,128)(2,1)}), bf16[128,32,256]{2,0,1:T(8,128)(2,1)}, u32[]{:S(2)}, u32[]{:S(2)}) async-start(bf16[128,32,256]{2,0,1:T(8,128)(2,1)} %bitcast.58), calls=%async_computation.1 | async-start | bytes 4194304 | tf_op jit(solution)/shard_map/all_to_all | solution.py:74
  29.0 2.1 copy-start.11
  29.0 407.2 %all-reduce.7.cloned.1.call-start = ((), (), s32[]{:S(2)}) async-start(), calls=%async_computation.3 | async-start | bytes 4194304 | tf_op jit(solution)/shard_map/psum | solution.py:61
  29.4 0.8 copy-start.5
  31.1 2.0 copy-start.4
  33.1 0.9 copy-start.9
  35.8 0.7 copy-start.16
  35.8 400.4 %copy-start.3 = (bf16[256,256]{1,0:T(8,128)(2,1)S(1)}, bf16[256,256]{1,0:T(8,128)(2,1)}, u32[]{:S(2)}) copy-start(bf16[256,256]{1,0:T(8,128)(2,1)} %param.19) | copy-start | bytes 393220
  35.8 583.9 %reduce-scatter.2.cloned.1.call-start = ((), (), s32[]{:S(2)}) async-start(), calls=%async_computation.4 | async-start | bytes 2162688 | tf_op jit(solution)/shard_map/reduce_scatter | solution.py:79
  442.6 1.3 copy-start.1
  446.0 173.6 %copy-start.7 = (bf16[256,256]{1,0:T(8,128)(2,1)S(1)}, bf16[256,256]{1,0:T(8,128)(2,1)}, u32[]{:S(2)}) copy-start(bf16[256,256]{1,0:T(8,128)(2,1)} %param.22) | copy-start | bytes 393220
  446.1 175.3 %copy-start.17 = (bf16[256]{0:T(256)(128)(2,1)S(1)}, bf16[256]{0:T(256)(128)(2,1)}, u32[]{:S(2)}) copy-start(bf16[256]{0:T(256)(128)(2,1)} %param.23) | copy-start | bytes 1540
  446.1 384.9 %all-to-all-start = ((bf16[32,128,256]{2,1,0:T(8,128)(2,1)}), bf16[32,128,256]{2,1,0:T(8,128)(2,1)}, u32[]{:S(2)}, u32[]{:S(2)}) async-start(bf16[32,128,256]{2,1,0:T(8,128)(2,1)} %bitcast.59), calls=%async_computation | async-start | bytes 4194304 | tf_op jit(solution)/shard_map/all_to_all | solution.py:67
  467.7 277.1 %all-gather.2.cloned.1.call-start = ((), (), s32[]{:S(2)}) async-start(), calls=%async_computation.5 | async-start | bytes 2162688 | tf_op jit(solution)/shard_map/all_gather | solution.py:89
  621.4 292.8 %all-reduce.9.cloned.1.call-start = ((), (), s32[]{:S(2)}) async-start(), calls=%async_computation.6 | async-start | bytes 524288 | tf_op jit(solution)/shard_map/psum | solution.py:112
  624.2 3.7 copy-start.2
  624.2 4.0 copy-start.10
  624.2 4.0 copy-start.18
  624.2 4.2 copy-start.6
Sparse Core Ops, SparseCore 0:
  35.9 400.1 all-reduce.6
  446.2 173.4 reduce-scatter.1
  623.8 74.0 all-gather.1
  747.9 166.1 all-reduce.8
where the time goes:
time: 924 us
  waiting for transfers between devices  632 us (68%)
  blocking collectives  193 us (21%)
  starting transfers between devices  40.3 us (4%)
  matrix products  30.5 us (3%)
  between operations  14.1 us (2%)
  local copies, waits for them, and re-layouts  12.5 us (1%)
    psum x1, waiting for transfers between devices, local(): low_rank = lax.psum(partial_value.astype(jnp.bfloat16), 'mp')  400 us
    reduce_scatter x1, waiting for transfers between devices, local(): lax.psum_scatter(contract_cols(d_lift_round, u_emb).astype(jnp.bfloat16),...  152 us
    psum x1, blocking collectives, local(): lax.psum((grad_wf, grad_bf, grad_ws, grad_bs, grad_vb, grad_ub, grad_bb),...  115 us
    psum x1, waiting for transfers between devices, local(): lax.psum(grad_v.astype(jnp.bfloat16), 'rep').astype(jnp.float32)  80.1 us
    psum x1, blocking collectives, local(): lax.psum(grad_table.astype(jnp.bfloat16), 'rep').astype(jnp.float32)  78.6 us
    all_to_all x1, starting transfers between devices, local(): lax.all_to_all(cross_local, 'mp', split_axis=0, concat_axis=1, tiled=True)  21.6 us
    all_to_all x1, starting transfers between devices, local(): lax.all_to_all(cot_cross, 'mp', split_axis=1, concat_axis=0, tiled=True)  18.5 us
  transfers between devices with their start and end apart: 6, of which 3 were waited for; matrix products, arithmetic and copies ran while one was open for 3% of the time, Pallas kernels for 0%

commit v1 on v0

--- a/solution.py
+++ b/solution.py
@@ -105,7 +105,7 @@
     grad_wf = grad_scale * contract_rows(dense_feats, d_first_round)
     grad_bf = grad_scale * jnp.sum(d_first, axis=0)
     dense_sums = lax.psum(
-        (grad_wf, grad_bf, grad_ws, grad_bs, grad_vb, grad_ub, grad_bb), ("rep", "mp")
+        lax.psum((grad_wf, grad_bf, grad_ws, grad_bs, grad_vb, grad_ub, grad_bb), "mp"), "rep"
     )
     table_sums = (
         lax.psum(grad_table.astype(jnp.bfloat16), "rep").astype(jnp.float32),

time: 924 us -> 1280 us (1.39)
  waiting for transfers between devices: 632 us -> 815 us
  blocking collectives: 193 us -> 360 us
    psum x0 -> x1, waiting for transfers between devices: none -> 174 us  [local(): lax.psum((grad_wf, grad_bf, grad_ws, grad_bs, grad_vb, grad_ub, grad_bb),...]
    psum x0 -> x1, blocking collectives: none -> 117 us  [local(): lax.psum(lax.psum((grad_wf, grad_bf, grad_ws, grad_bs, grad_vb, grad_ub,...]
    psum x1, blocking collectives: 115 us -> 165 us  [local(): lax.psum((grad_wf, grad_bf, grad_ws, grad_bs, grad_vb, grad_ub, grad_bb),...]
  transfers between devices with their start and end apart: 6 -> 7, of which waited for: 3 -> 4; matrix products, arithmetic and copies ran while one was open for 3% -> 2% of each run, Pallas kernels for 0% -> 0%
where the time goes in v1:
time: 1280 us
  waiting for transfers between devices  815 us (64%)
  blocking collectives  360 us (28%)
  starting transfers between devices  40.3 us (3%)
  matrix products  32.3 us (3%)
  between operations  14 us (1%)
    psum x1, waiting for transfers between devices, local(): low_rank = lax.psum(partial_value.astype(jnp.bfloat16), 'mp')  402 us
    psum x1, waiting for transfers between devices, local(): lax.psum((grad_wf, grad_bf, grad_ws, grad_bs, grad_vb, grad_ub, grad_bb),...  174 us
    psum x1, blocking collectives, local(): lax.psum((grad_wf, grad_bf, grad_ws, grad_bs, grad_vb, grad_ub, grad_bb),...  165 us
    reduce_scatter x1, waiting for transfers between devices, local(): lax.psum_scatter(contract_cols(d_lift_round, u_emb).astype(jnp.bfloat16),...  149 us
    psum x1, blocking collectives, local(): lax.psum(lax.psum((grad_wf, grad_bf, grad_ws, grad_bs, grad_vb, grad_ub,...  117 us
    psum x1, waiting for transfers between devices, local(): lax.psum(grad_v.astype(jnp.bfloat16), 'rep').astype(jnp.float32)  90 us
    psum x1, blocking collectives, local(): lax.psum(grad_table.astype(jnp.bfloat16), 'rep').astype(jnp.float32)  78.1 us
  transfers between devices with their start and end apart: 7, of which 4 were waited for; matrix products, arithmetic and copies ran while one was open for 2% of the time, Pallas kernels for 0%

profile of v1, /device:TPU:8, one launch (start us, length us, event | category | flops | bytes accessed | tf_op | source)
XLA Modules:
  0.0 1275.1 jit_solution(11124720484701194761)
XLA Ops:
  7.2 0.0 copy-start
  7.2 3.2 copy.33
  10.4 0.0 copy-start.6
  10.4 18.5 %all-to-all-start.1 = ((bf16[128,32,256]{2,0,1:T(8,128)(2,1)}), bf16[128,32,256]{2,0,1:T(8,128)(2,1)}, u32[]{:S(2)}, u32[]{:S(2)}) async-start(bf16[128,32,256]{2,0,1:T(8,128)(2,1)} %bitcast.58), calls=%async_computation.1 | async-start | bytes 4194304 | tf_op jit(solution)/shard_map/all_to_all | solution.py:74
  29.0 0.0 copy-start.8
  29.0 0.0 all-reduce.10.cloned.1.call-start
  29.0 0.0 copy-done.12
  29.1 0.0 copy-done.11
  29.1 0.0 copy-done.9
  29.1 0.0 copy-done.10
  29.1 0.2 convolution_add_fusion.2
  29.4 0.0 copy-done
  29.4 0.0 copy-done.6
  29.4 0.9 fusion.22
  30.3 0.0 copy-done.8
  30.3 2.0 convolution_convert_fusion.1
  32.3 0.0 copy-done.4
  32.4 0.0 copy-start.7
  32.4 0.7 fusion.35
  33.1 0.2 copy-done.7
  33.3 0.2 fusion.8
  33.4 1.5 convert_element_type.134
  35.0 0.0 all-reduce.10.cloned.1.call-update
  35.0 0.0 reduce-scatter.2.cloned.1.call-start
  35.0 0.6 copy-done.13
  35.6 402.2 %all-reduce.10.cloned.1.call-done = bf16[4096,256]{1,0:T(8,128)(2,1)} async-done(((bf16[4096,256]{1,0:T(8,128)(2,1)}), bf16[4096,256]{1,0:T(8,128)(2,1)}) %all-reduce.10.cloned.1.call-update) | async-done | bytes 2097168 | tf_op jit(solution)/shard_map/psum | solution.py:61
  437.8 0.0 all-to-all-done.1
  437.8 6.4 bitcast_multiply_fusion
  444.3 1.4 copy-done.1
  445.6 2.1 convolution_convert_fusion
  447.7 0.0 reduce-scatter.2.cloned.1.call-update
  447.7 0.0 copy-start.14
  447.7 0.0 copy-start.5
  447.8 21.6 %all-to-all-start = ((bf16[32,128,256]{2,1,0:T(8,128)(2,1)}), bf16[32,128,256]{2,1,0:T(8,128)(2,1)}, u32[]{:S(2)}, u32[]{:S(2)}) async-start(bf16[32,128,256]{2,1,0:T(8,128)(2,1)} %bitcast.59), calls=%async_computation | async-start | bytes 4194304 | tf_op jit(solution)/shard_map/all_to_all | solution.py:67
  469.4 0.0 all-reduce.12.cloned.1.call-start
  469.4 0.0 copy-done.14
  469.4 1.8 convolution_multiply_fusion.2
  471.2 0.0 copy-done.5
  471.2 1.7 fusion.21
  472.9 148.6 %reduce-scatter.2.cloned.1.call-done = bf16[128,256]{1,0:T(8,128)(2,1)} async-done(((bf16[4096,256]{1,0:T(8,128)(2,1)}), bf16[128,256]{1,0:T(8,128)(2,1)}) %reduce-scatter.2.cloned.1.call-update) | async-done | bytes 65552 | tf_op jit(solution)/shard_map/reduce_scatter | solution.py:79
  621.5 1.1 fusion.11
  622.6 0.0 copy-start.2
  622.6 0.9 convolution_multiply_fusion.3
  623.5 1.3 fusion.34
  624.8 1.3 convolution_multiply_fusion
  626.1 0.0 all-reduce.12.cloned.1.call-update
  626.2 0.0 all-gather.2.cloned.1.call-start
  626.2 0.5 all-gather.2.cloned.1.call-update
  626.7 0.0 all-reduce.14.cloned.1.call-start
  626.8 3.6 fusion.7
  630.4 0.4 fusion.33
  630.8 0.2 fusion.13
  631.0 165.3 %all-reduce = (f32[256]{0:T(256)S(1)}, f32[13,1024]{1,0:T(8,128)S(1)}, f32[1024]{0:T(1024)S(1)}, f32[256]{0:T(256)S(1)}) all-reduce(f32[256]{0:T(256)S(1)} %broadcast_multiply_fusion.2, f32[13,1024]{1,0:T(8,128)S(1)} %fusion.13, f32[1024]{0:T(1024)S(1)} %broadcast_multiply_fusion, ...), channel_id=1, replica_groups=mesh['rep'=16,'mp'=32] {'mp'}, use_global_device_ids=true, to_apply=%region_12.13 | all-reduce | flops 14848 | bytes 118784 | tf_op jit(solution)/shard_map/psum | solution.py:108
  796.2 173.8 %all-reduce.12.cloned.1.call-done = (f32[256,256]{1,0:T(8,128)}, f32[256,256]{1,0:T(8,128)}, f32[1024,256]{1,0:T(8,128)}) async-done(((f32[256,256]{1,0:T(8,128)}, f32[256,256]{1,0:T(8,128)}, f32[1024,256]{1,0:T(8,128)}), (f32[256,256]{1,0:T(8,128)}, f32[256,256]{1,0:T(8,128)}, f32[1024,256]{1,0:T(8,128)})) %all-reduce.12.cloned.1.call-update) | async-done | bytes 1572880 | tf_op jit(solution)/shard_map/psum | solution.py:108
  970.0 116.6 %all-reduce.15 = (bf16[256,256]{1,0:T(8,128)(2,1)}, bf16[256,256]{1,0:T(8,128)(2,1)}, bf16[256]{0:T(256)(128)(2,1)}, bf16[13,1024]{1,0:T(8,128)(2,1)}, bf16[1024...) all-reduce(f32[256,256]{1,0:T(8,128)} %get-tuple-element.17, ...), channel_id=1, replica_groups=mesh['rep'=16,'mp'=32] {'rep'}, use_global_device_ids=true, to_apply=%region_8.9 | all-reduce | flops 408064 | bytes 2448384 | tf_op jit(solution)/shard_map/psum | solution.py:107
  1086.6 3.0 fusion.6
  1089.6 0.0 all-reduce.14.cloned.1.call-update
  1089.6 4.5 fusion.15
  1094.1 78.1 %all-reduce.3 = (bf16[1,64,256]{2,1,0:T(8,128)(2,1)}, bf16[256]{0:T(256)(128)(2,1)}) all-reduce(bf16[1,64,256]{2,1,0:T(8,128)(2,1)S(1)} %fusion.15, bf16[256]{0:T(256)(128)(2,1)S(1)} %multiply_convert_fusion.2), channel_id=1, replica_groups=mesh['rep'=16,'mp'=32] {'rep'}, use_global_device_ids=true, to_apply=%region_2.3 | all-reduce | flops 16640 | bytes 66560 | tf_op jit(solution)/shard_map/psum | solution.py:111
  1172.2 0.0 all-to-all-done
  1172.2 3.1 copy.31
  1175.4 90.0 %all-reduce.14.cloned.1.call-done = (bf16[256,256]{1,0:T(8,128)(2,1)}, bf16[256,256]{1,0:T(8,128)(2,1)}) async-done(((bf16[256,256]{1,0:T(8,128)(2,1)}, bf16[256,256]{1,0:T(8,128)(2,1)}), (bf16[256,256]{1,0:T(8,128)(2,1)}, bf16[256,256]{1,0:T(8,128)(2,1)})) %all-reduce.14.cloned.1.call-update) | async-done | bytes 262160 | tf_op jit(solution)/shard_map/psum | solution.py:112
  1265.4 1.6 copy.55
  1267.0 1.6 copy.56
  (19 shorter events, 0.0 us)
Async XLA Ops:
  7.2 22.2 %copy-start = (bf16[1024,256]{1,0:T(8,128)(2,1)S(1)}, bf16[1024,256]{1,0:T(8,128)(2,1)}, u32[]{:S(2)}) copy-start(bf16[1024,256]{1,0:T(8,128)(2,1)} %param.26) | copy-start | bytes 1572868
  10.4 18.6 %copy-start.12 = (bf16[256]{0:T(256)(128)(2,1)S(1)}, bf16[256]{0:T(256)(128)(2,1)}, u32[]{:S(2)}) copy-start(bf16[256]{0:T(256)(128)(2,1)} %param.27) | copy-start | bytes 1540
  10.4 18.6 %copy-start.11 = (bf16[1024]{0:T(1024)(128)(2,1)S(1)}, bf16[1024]{0:T(1024)(128)(2,1)}, u32[]{:S(2)}) copy-start(bf16[1024]{0:T(1024)(128)(2,1)} %param.25) | copy-start | bytes 6148
  10.4 18.7 %copy-start.9 = (bf16[13,1024]{1,0:T(8,128)(2,1)S(1)}, bf16[13,1024]{1,0:T(8,128)(2,1)}, u32[]{:S(2)}) copy-start(bf16[13,1024]{1,0:T(8,128)(2,1)} %param.24) | copy-start | bytes 79876
  10.4 18.7 %copy-start.10 = (bf16[128,13]{0,1:T(8,128)(2,1)S(1)}, bf16[128,13]{0,1:T(8,128)(2,1)}, u32[]{:S(2)}) copy-start(bf16[128,13]{0,1:T(8,128)(2,1)} %param.15) | copy-start | bytes 9988
  10.4 18.9 %copy-start.6 = (bf16[128,256]{1,0:T(8,128)(2,1)S(1)}, bf16[128,256]{1,0:T(8,128)(2,1)}, u32[]{:S(2)}) copy-start(bf16[128,256]{1,0:T(8,128)(2,1)} %param.29) | copy-start | bytes 196612
  10.4 427.4 %all-to-all-start.1 = ((bf16[128,32,256]{2,0,1:T(8,128)(2,1)}), bf16[128,32,256]{2,0,1:T(8,128)(2,1)}, u32[]{:S(2)}, u32[]{:S(2)}) async-start(bf16[128,32,256]{2,0,1:T(8,128)(2,1)} %bitcast.58), calls=%async_computation.1 | async-start | bytes 4194304 | tf_op jit(solution)/shard_map/all_to_all | solution.py:74
  29.0 1.4 copy-start.8
  29.0 408.8 %all-reduce.10.cloned.1.call-start = ((), (), s32[]{:S(2)}) async-start(), calls=%async_computation.3 | async-start | bytes 4194304 | tf_op jit(solution)/shard_map/psum | solution.py:61
  30.3 2.0 copy-start.4
  32.4 0.9 copy-start.7
  35.0 0.7 copy-start.13
  35.0 402.9 %copy-start.3 = (bf16[256,256]{1,0:T(8,128)(2,1)S(1)}, bf16[256,256]{1,0:T(8,128)(2,1)}, u32[]{:S(2)}) copy-start(bf16[256,256]{1,0:T(8,128)(2,1)} %param.19) | copy-start | bytes 393220
  35.0 586.5 %reduce-scatter.2.cloned.1.call-start = ((), (), s32[]{:S(2)}) async-start(), calls=%async_computation.4 | async-start | bytes 2162688 | tf_op jit(solution)/shard_map/reduce_scatter | solution.py:79
  444.3 1.4 copy-start.1
  447.7 21.7 %copy-start.14 = (bf16[256]{0:T(256)(128)(2,1)S(1)}, bf16[256]{0:T(256)(128)(2,1)}, u32[]{:S(2)}) copy-start(bf16[256]{0:T(256)(128)(2,1)} %param.23) | copy-start | bytes 1540
  447.7 23.5 %copy-start.5 = (bf16[256,256]{1,0:T(8,128)(2,1)S(1)}, bf16[256,256]{1,0:T(8,128)(2,1)}, u32[]{:S(2)}) copy-start(bf16[256,256]{1,0:T(8,128)(2,1)} %param.22) | copy-start | bytes 393220
  447.8 724.5 %all-to-all-start = ((bf16[32,128,256]{2,1,0:T(8,128)(2,1)}), bf16[32,128,256]{2,1,0:T(8,128)(2,1)}, u32[]{:S(2)}, u32[]{:S(2)}) async-start(bf16[32,128,256]{2,1,0:T(8,128)(2,1)} %bitcast.59), calls=%async_computation | async-start | bytes 4194304 | tf_op jit(solution)/shard_map/all_to_all | solution.py:67
  469.4 500.7 %all-reduce.12.cloned.1.call-start = ((), (), s32[]{:S(2)}) async-start(), calls=%async_computation.6 | async-start | bytes 3145728 | tf_op jit(solution)/shard_map/psum | solution.py:108
  622.6 3.6 copy-start.2
  626.2 460.5 %all-gather.2.cloned.1.call-start = ((), (), s32[]{:S(2)}) async-start(), calls=%async_computation.5 | async-start | bytes 2162688 | tf_op jit(solution)/shard_map/all_gather | solution.py:89
  626.7 638.7 %all-reduce.14.cloned.1.call-start = ((), (), s32[]{:S(2)}) async-start(), calls=%async_computation.7 | async-start | bytes 524288 | tf_op jit(solution)/shard_map/psum | solution.py:112
Sparse Core Ops, SparseCore 0:
  35.1 402.6 all-reduce.9
  447.8 173.5 reduce-scatter.1
  626.3 343.7 all-reduce.11
  973.6 87.4 all-gather.1
  1089.8 175.5 all-reduce.13
